TPU v7x, 32 devices: a whole 2x2x4 slice. The times are simulated.
32 devices in a mesh: wide: 8 (over y, x, core), narrow: 4 (over z).
Axes of the slice: x: 2, y: 2, z: 4, core: 2. Of those that a mesh axis runs over, the one named last changes fastest.
Arguments:
- row_vectors: bfloat16 [8192, 2048], P('wide'), may hold values from -0.59765625 to 1.3984375
- col_vectors: bfloat16 [2048, 2048], P('narrow', 'wide'), may hold values from -0.59765625 to 1.3984375
- primal_matrix: bfloat16 [2048, 2048], P('wide'), may hold values from -1 to 3, as said below
- dual_inverse: bfloat16 [2048, 2048], P('wide'), may hold values from -1 to 3, as said below
Outputs:
- factored: float32 [8192, 2048], P('wide', 'narrow')
Inputs may be any that keep to these rules, and one draw needn't show every extreme that they name: `primal_matrix`: symmetric positive definite. `dual_inverse`: symmetric positive definite.
All inputs are finite; a program needn't handle non-finite values.
Results may differ from a plain program's by a relative error of at most 0.0027.
Values may be sent and summed in bfloat16 or wider, within the bound.
No kernel may reach another device: no remote copies, remote signals or barrier semaphores. Data moves between devices by JAX's collectives and lax.ppermute only.
A program may use at most 64 MiB of HBM per device.

v0:
```python
import jax
import jax.numpy as jnp
from jax import lax
from jax.sharding import PartitionSpec as P


def spread(value, axis, source):
    kept = jnp.where(lax.axis_index(axis) == source, value, 0).astype(value.dtype)
    return lax.psum(kept, axis)


def per_device(row_vectors, col_vectors, primal_matrix, dual_inverse):
    wide_count = lax.axis_size("wide")
    wide_index = lax.axis_index("wide")
    narrow_index = lax.axis_index("narrow")
    cone_order = primal_matrix.shape[1]
    panel_width = col_vectors.shape[0]
    panel_share = panel_width // wide_count
    gram_scale = 16.0 / (cone_order * cone_order)
    column_set = lax.all_gather(col_vectors, "wide", axis=1, tiled=True)
    local_panel = lax.dynamic_slice_in_dim(column_set, wide_index * panel_share, panel_share, 0)
    panel_set = spread(local_panel, "narrow", 0)
    prod_primal = jnp.dot(primal_matrix, column_set.T, preferred_element_type=jnp.float32).astype(
        jnp.bfloat16
    )
    prod_dual = jnp.dot(dual_inverse, column_set.T, preferred_element_type=jnp.float32).astype(
        jnp.bfloat16
    )
    pieces = (
        lax.all_gather(prod_primal, "wide", axis=0, tiled=True),
        lax.all_gather(prod_dual, "wide", axis=0, tiled=True),
    )
    row_slice = row_vectors
    panel_slice = panel_set
    gram_primal = jnp.dot(row_slice, pieces[0], preferred_element_type=jnp.float32)
    gram_dual = jnp.dot(row_slice, pieces[1], preferred_element_type=jnp.float32)
    tile_primal = jnp.dot(panel_slice, pieces[0], preferred_element_type=jnp.float32)
    tile_dual = jnp.dot(panel_slice, pieces[1], preferred_element_type=jnp.float32)
    slab = gram_primal * gram_dual * gram_scale
    panel_tile = tile_primal * tile_dual * gram_scale
    gram = lax.all_gather(panel_tile, "wide", axis=0, tiled=True)
    panel_primal, panel_dual = (spread(prod_primal, "narrow", 0), spread(prod_dual, "narrow", 0))
    pieces = (
        lax.all_gather(panel_primal, "wide", axis=0, tiled=True),
        lax.all_gather(panel_dual, "wide", axis=0, tiled=True),
    )
    row_slice = row_vectors
    panel_slice = panel_set
    first_primal = jnp.dot(row_slice, pieces[0], preferred_element_type=jnp.float32)
    first_dual = jnp.dot(row_slice, pieces[1], preferred_element_type=jnp.float32)
    diag_primal = jnp.dot(panel_slice, pieces[0], preferred_element_type=jnp.float32)
    diag_dual = jnp.dot(panel_slice, pieces[1], preferred_element_type=jnp.float32)
    slab_first = first_primal * first_dual * gram_scale
    diag_share = diag_primal * diag_dual * gram_scale
    diag_block = lax.all_gather(diag_share, "wide", axis=0, tiled=True)
    factor = jnp.linalg.cholesky(diag_block)
    panel_cols = jax.scipy.linalg.solve_triangular(factor, slab_first.T, lower=True).T
    solved = jax.scipy.linalg.solve_triangular(factor, gram, lower=True)
    trailing = slab - jnp.dot(panel_cols, solved, precision=lax.Precision.HIGHEST)
    return jnp.where(narrow_index == 0, panel_cols, trailing)


def solution(mesh):
    placed = (P("wide", None), P("narrow", "wide"), P("wide", None), P("wide", None))
    return jax.shard_map(
        per_device, mesh=mesh, in_specs=placed, out_specs=P("wide", "narrow"), check_vma=False
    )
```

profile of v0, /device:TPU:0, one launch (start us, length us, event | category | flops | bytes accessed | tf_op | source)
XLA Modules:
  0.0 404.9 jit_solution(14323535029194417202)
XLA Ops:
  7.3 32.8 %all-gather.8.cloned.1.call-done = bf16[512,2048]{1,0:T(8,128)(2,1)} async-done(((bf16[512,256]{1,0:T(8,128)(2,1)}), bf16[512,2048]{1,0:T(8,128)(2,1)}) %all-gather.8.cloned.1.call-update) | async-done | bytes 2097168 | tf_op jit(solution)/shard_map/all_gather | solution.py:20
  40.1 3.3 broadcast_select_fusion.1
  45.8 44.0 %all-reduce.4.cloned.1.call-done = (bf16[256,512]{1,0:T(8,128)(2,1)}, bf16[256,512]{1,0:T(8,128)(2,1)}, bf16[64,2048]{1,0:T(8,128)(2,1)}) async-done(((bf16[256,512]{1,0:T(8,128)(2,1)}, bf16[256,512]{1,0:T(8,128)(2,1)}, bf16[64,2048]{1,0:T(8,128)(2,1)}), (bf16[256,512]{1,0:T(8,128)(2,1)}, bf16[256,512]{1,0:T(8,128)(2,1)}, bf16[64,2048]{1,0:T(8,128)(2,1)})) %all-reduce.4.cloned.1.call-update) | async-done | bytes 786448 | tf_op jit(solution)/shard_map/psum | solution.py:9
  91.6 27.0 %all-gather.10.cloned.1.call-done = bf16[2048,512]{1,0:T(8,128)(2,1)} async-done(((bf16[256,512]{1,0:T(8,128)(2,1)}), bf16[2048,512]{1,0:T(8,128)(2,1)}) %all-gather.10.cloned.1.call-update) | async-done | bytes 2097168 | tf_op jit(solution)/shard_map/all_gather | solution.py:44
  118.7 2.2 fusion.65
  120.9 27.4 %all-gather.12.cloned.1.call-done = bf16[2048,512]{1,0:T(8,128)(2,1)} async-done(((bf16[256,512]{1,0:T(8,128)(2,1)}), bf16[2048,512]{1,0:T(8,128)(2,1)}) %all-gather.12.cloned.1.call-update) | async-done | bytes 2097168 | tf_op jit(solution)/shard_map/all_gather | solution.py:45
  148.2 2.7 fusion.12
  151.2 26.6 %all-gather.16.cloned.1.call-done = bf16[2048,512]{1,0:T(8,128)(2,1)} async-done(((bf16[256,512]{1,0:T(8,128)(2,1)}), bf16[2048,512]{1,0:T(8,128)(2,1)}) %all-gather.16.cloned.1.call-update) | async-done | bytes 2097168 | tf_op jit(solution)/shard_map/all_gather | solution.py:30
  177.8 2.2 fusion.68
  180.0 27.3 %all-gather.18.cloned.1.call-done = bf16[2048,512]{1,0:T(8,128)(2,1)} async-done(((bf16[256,512]{1,0:T(8,128)(2,1)}), bf16[2048,512]{1,0:T(8,128)(2,1)}) %all-gather.18.cloned.1.call-update) | async-done | bytes 2097168 | tf_op jit(solution)/shard_map/all_gather | solution.py:31
  207.3 2.7 fusion.11
  210.1 6.0 %fusion.67 = f32[512,1024]{1,0:T(8,128)} fusion(bf16[2048,512]{1,0:T(8,128)(2,1)S(1)} %copy-done.8, bf16[1024,2048]{1,0:T(8,128)(2,1)} %param.4), kind=kOutput, calls=%fused_computation.112 | convolution fusion | flops 2147483648 | bytes 8388608 | tf_op jit(solution)/shard_map/dot_general | solution.py:35
  216.1 2.4 fusion.66
  218.6 3.7 multiply_multiply_fusion
  222.3 10.4 %all-gather.14.cloned.1.call-done = f32[512,512]{1,0:T(8,128)} async-done(((f32[64,512]{1,0:T(8,128)}), f32[512,512]{1,0:T(8,128)}) %all-gather.14.cloned.1.call-update) | async-done | bytes 1048592 | tf_op jit(solution)/shard_map/all_gather | solution.py:55
  235.5 11.9 %cholesky.104 = f32[128,128]{1,0:T(8,128)S(1)} custom-call(f32[128,128]{1,0:T(8,128)S(1)} %cholesky.266), custom_call_target="Cholesky" | custom-call | tf_op jit(solution)/shard_map/jit(cholesky)/cholesky | solution.py:56
  247.6 9.8 %custom-call.34 = f32[1,128,128]{1,2,0:T(8,128)S(1)} custom-call(f32[1,128,128]{2,1,0:T(8,128)S(1)} %get-tuple-element.35), custom_call_target="InvertDiagBlocksLowerTriangular" | custom-call | tf_op jit(solution)/shard_map/jit(cholesky)/cholesky | solution.py:56
  259.9 11.7 %cholesky.217 = f32[128,128]{1,0:T(8,128)S(1)} custom-call(f32[128,128]{1,0:T(8,128)S(1)} %cholesky.270), custom_call_target="Cholesky" | custom-call | tf_op jit(solution)/shard_map/jit(cholesky)/cholesky | solution.py:56
  271.7 9.8 %custom-call.35 = f32[1,128,128]{1,2,0:T(8,128)S(1)} custom-call(f32[1,128,128]{2,1,0:T(8,128)S(1)} %get-tuple-element.32), custom_call_target="InvertDiagBlocksLowerTriangular" | custom-call | tf_op jit(solution)/shard_map/jit(cholesky)/cholesky | solution.py:56
  283.1 12.1 %cholesky.238 = f32[128,128]{1,0:T(8,128)S(1)} custom-call(f32[128,128]{1,0:T(8,128)S(1)} %cholesky.275), custom_call_target="Cholesky" | custom-call | tf_op jit(solution)/shard_map/jit(cholesky)/cholesky | solution.py:56
  295.2 9.8 %custom-call.36 = f32[1,128,128]{1,2,0:T(8,128)S(1)} custom-call(f32[1,128,128]{2,1,0:T(8,128)S(1)} %get-tuple-element.29), custom_call_target="InvertDiagBlocksLowerTriangular" | custom-call | tf_op jit(solution)/shard_map/jit(cholesky)/cholesky | solution.py:56
  306.5 11.7 %cholesky.255 = f32[128,128]{1,0:T(8,128)S(1)} custom-call(f32[128,128]{1,0:T(8,128)S(1)} %convolution_subtract_fusion.7), custom_call_target="Cholesky" | custom-call | tf_op jit(solution)/shard_map/jit(cholesky)/cholesky | solution.py:56
  323.1 10.8 %while.1 = (s32[]{:T(128)}, f32[512,512]{1,0:T(8,128)S(1)}, s32[4,2]{0,1:T(2,128)S(1)}, f32[4,128,128]{2,1,0:T(8,128)}, s32[]{:T(128)}) while((s32[]{:T(128)}, f32[512,512]{1,0:T(8,128)S(1)}, s32[4,2]{0,1:T(2,128)S(1)}, f32[4,128,128]{2,1,0:T(8,128)}, s32[]{:T(128)}) %tuple.29), condition=%wide.while_cond, body=%wide.while_body.sunk | while | flops 2 | bytes 132205 | solution.py:57
  323.8 2.0 bitcast_dynamic-update-slice_fusion.2
  326.5 2.0 bitcast_dynamic-update-slice_fusion.2
  329.2 2.0 bitcast_dynamic-update-slice_fusion.2
  331.9 2.0 bitcast_dynamic-update-slice_fusion.2
  333.9 40.3 %custom-call.37 = f32[4,128,128]{1,2,0:T(8,128)S(1)} custom-call(f32[4,128,128]{2,1,0:T(8,128)} %get-tuple-element.12), custom_call_target="InvertDiagBlocksLowerTriangular" | custom-call | tf_op jit(solution)/shard_map/jit(_solve_triangular)/triangular_solve | solution.py:57
  374.2 1.8 fusion.29
  387.5 3.6 fusion.10
  391.1 3.8 fusion
  395.0 2.9 copy.14
  (99 shorter events, 30.0 us)
Async XLA Ops:
  6.5 33.5 %copy-start = (bf16[256,2048]{1,0:T(8,128)(2,1)S(1)}, bf16[256,2048]{1,0:T(8,128)(2,1)}, u32[]{:S(2)}) copy-start(bf16[256,2048]{1,0:T(8,128)(2,1)} %param.6) | copy-start | bytes 3145732
  6.5 36.8 %copy-start.16 = (bf16[256,2048]{1,0:T(8,128)(2,1)S(1)}, bf16[256,2048]{1,0:T(8,128)(2,1)}, u32[]{:S(2)}) copy-start(bf16[256,2048]{1,0:T(8,128)(2,1)} %param.7) | copy-start | bytes 3145732
  6.5 33.5 %all-gather.8.cloned.1.call-start = ((), (), s32[]{:S(2)}) async-start(), calls=%async_computation | async-start | bytes 2359296 | tf_op jit(solution)/shard_map/all_gather | solution.py:20
  7.3 82.6 %all-reduce.4.cloned.1.call-start = ((), (), s32[]{:S(2)}) async-start(), calls=%async_computation.7 | async-start | bytes 1572864 | tf_op jit(solution)/shard_map/psum | solution.py:9
  40.1 3.3 copy-start.13
  45.7 73.0 %all-gather.10.cloned.1.call-start = ((), (), s32[]{:S(2)}) async-start(), calls=%async_computation.1 | async-start | bytes 2359296 | tf_op jit(solution)/shard_map/all_gather | solution.py:44
  89.8 58.4 %copy-start.1 = (bf16[64,2048]{1,0:T(8,128)(2,1)S(1)}, bf16[64,2048]{1,0:T(8,128)(2,1)}, u32[]{:S(2)}) copy-start(bf16[64,2048]{1,0:T(8,128)(2,1)} %get-tuple-element.23) | copy-start | bytes 786436
  89.9 58.4 %all-gather.12.cloned.1.call-start = ((), (), s32[]{:S(2)}) async-start(), calls=%async_computation.2 | async-start | bytes 2359296 | tf_op jit(solution)/shard_map/all_gather | solution.py:45
  90.4 87.3 %all-gather.16.cloned.1.call-start = ((), (), s32[]{:S(2)}) async-start(), calls=%async_computation.4 | async-start | bytes 2359296 | tf_op jit(solution)/shard_map/all_gather | solution.py:30
  91.0 116.3 %all-gather.18.cloned.1.call-start = ((), (), s32[]{:S(2)}) async-start(), calls=%async_computation.5 | async-start | bytes 2359296 | tf_op jit(solution)/shard_map/all_gather | solution.py:31
  91.6 141.0 %all-gather.14.cloned.1.call-start = ((), (), s32[]{:S(2)}) async-start(), calls=%async_computation.3 | async-start | bytes 1179648 | tf_op jit(solution)/shard_map/all_gather | solution.py:55
  151.0 231.3 %all-gather.20.cloned.1.call-start = ((), (), s32[]{:S(2)}) async-start(), calls=%async_computation.6 | async-start | bytes 1179648 | tf_op jit(solution)/shard_map/all_gather | solution.py:41
  177.8 32.3 %copy-start.8 = (bf16[2048,512]{1,0:T(8,128)(2,1)S(1)}, bf16[2048,512]{1,0:T(8,128)(2,1)}, u32[]{:S(2)}) copy-start(bf16[2048,512]{1,0:T(8,128)(2,1)} %all-gather.16.cloned.1.call-done) | copy-start | bytes 6291460
  210.1 6.0 %copy-start.7 = (bf16[2048,512]{1,0:T(8,128)(2,1)S(1)}, bf16[2048,512]{1,0:T(8,128)(2,1)}, u32[]{:S(2)}) copy-start(bf16[2048,512]{1,0:T(8,128)(2,1)} %all-gather.10.cloned.1.call-done) | copy-start | bytes 6291460
  210.1 6.0 %copy-start.14 = (bf16[1024,2048]{1,0:T(8,128)(2,1)S(1)}, bf16[1024,2048]{1,0:T(8,128)(2,1)}, u32[]{:S(2)}) copy-start(bf16[1024,2048]{1,0:T(8,128)(2,1)} %param.4) | copy-start | bytes 12582916
  216.1 2.4 copy-start.5
  232.6 1.7 copy-start.2
  234.5 1.0 copy-start.3
  374.2 4.1 %copy-start.6 = (f32[512,1024]{1,0:T(8,128)S(1)}, f32[512,1024]{1,0:T(8,128)}, u32[]{:S(2)}) copy-start(f32[512,1024]{1,0:T(8,128)} %multiply_multiply_fusion) | copy-start | bytes 6291460
  379.7 1.1 copy-start.9
  382.3 3.2 copy-start.11
  385.1 2.4 copy-start.10
  385.1 2.4 copy-start.12
  386.4 4.7 %copy-start.17 = (f32[512,1024]{1,0:T(8,128)S(1)}, f32[512,1024]{1,0:T(8,128)}, u32[]{:S(2)}) copy-start(f32[512,1024]{1,0:T(8,128)} %fusion.67) | copy-start | bytes 6291460
  387.5 3.7 copy-start.4
  387.5 3.7 copy-start.15
Sparse Core Ops, SparseCore 0:
  9.2 30.8 all-gather.7
  45.9 43.9 all-reduce.3
  91.7 26.9 all-gather.9
  120.4 27.7 all-gather.11
  150.0 27.7 all-gather.15
  179.5 27.7 all-gather.17
  209.2 23.3 all-gather.13
  234.5 23.5 all-gather.19
where the time goes:
time: 408 us; the launch traced here: 405 us
  waiting for transfers between devices  198 us (49%)
  other arithmetic  120 us (29%)
  matrix products  52.8 us (13%)
  between operations  16.8 us (4%)
  local copies, waits for them, and re-layouts  16.5 us (4%)
    another operation x14, other arithmetic, per_device(): factor = jnp.linalg.cholesky(diag_block)  79.1 us
    psum x1, waiting for transfers between devices, spread(): return lax.psum(kept, axis)  44 us
    another operation x3, other arithmetic, per_device(): jax.scipy.linalg.solve_triangular(factor, slab_first.T, lower=True)  40.4 us
    all_gather x1, waiting for transfers between devices, per_device(): column_set = lax.all_gather(col_vectors, 'wide', axis=1, tiled=True)  32.8 us
    all_gather x1, waiting for transfers between devices, per_device(): lax.all_gather(panel_dual, 'wide', axis=0, tiled=True)  27.4 us
    all_gather x1, waiting for transfers between devices, per_device(): lax.all_gather(prod_dual, 'wide', axis=0, tiled=True)  27.3 us
    all_gather x1, waiting for transfers between devices, per_device(): lax.all_gather(panel_primal, 'wide', axis=0, tiled=True)  27 us
    all_gather x1, waiting for transfers between devices, per_device(): lax.all_gather(prod_primal, 'wide', axis=0, tiled=True)  26.6 us
  transfers between devices with their start and end apart: 8, of which 7 were waited for; matrix products, arithmetic and copies ran while one was open for 41% of the time, Pallas kernels for 0%

commit v1 on v0

--- a/solution.py
+++ b/solution.py
@@ -6,7 +6,7 @@
 
 def spread(value, axis, source):
     kept = jnp.where(lax.axis_index(axis) == source, value, 0).astype(value.dtype)
-    return lax.psum(kept, axis)
+    return jnp.sum(lax.all_gather(kept, axis), axis=0)
 
 
 def per_device(row_vectors, col_vectors, primal_matrix, dual_inverse):

time: 408 us -> 448 us (1.098)
  waiting for transfers between devices: 198 us -> 231 us
  other arithmetic: 120 us -> 126 us
    all_gather x0 -> x3, waiting for transfers between devices: none -> 76.2 us  [spread(): return jnp.sum(lax.all_gather(kept, axis), axis=0)]
    psum x1 -> x0, waiting for transfers between devices: 44 us -> none  [spread(): return lax.psum(kept, axis)]
    reduce_sum x0 -> x3, other arithmetic: none -> 5.7 us  [spread(): return jnp.sum(lax.all_gather(kept, axis), axis=0)]
  transfers between devices with their start and end apart: 8 -> 10, of which waited for: 7 -> 9; matrix products, arithmetic and copies ran while one was open for 41% -> 40% of each run, Pallas kernels for 0% -> 0%
where the time goes in v1:
time: 448 us; the launch traced here: 444 us
  waiting for transfers between devices  231 us (52%)
  other arithmetic  126 us (28%)
  matrix products  53.8 us (12%)
  between operations  16.7 us (4%)
  local copies, waits for them, and re-layouts  16.3 us (4%)
    another operation x14, other arithmetic, per_device(): factor = jnp.linalg.cholesky(diag_block)  79 us
    all_gather x3, waiting for transfers between devices, spread(): return jnp.sum(lax.all_gather(kept, axis), axis=0)  76.2 us
    another operation x3, other arithmetic, per_device(): jax.scipy.linalg.solve_triangular(factor, slab_first.T, lower=True)  40.4 us
    all_gather x1, waiting for transfers between devices, per_device(): column_set = lax.all_gather(col_vectors, 'wide', axis=1, tiled=True)  32.8 us
    all_gather x1, waiting for transfers between devices, per_device(): lax.all_gather(panel_primal, 'wide', axis=0, tiled=True)  27.5 us
    all_gather x1, waiting for transfers between devices, per_device(): lax.all_gather(panel_dual, 'wide', axis=0, tiled=True)  27.5 us
    all_gather x1, waiting for transfers between devices, per_device(): lax.all_gather(prod_dual, 'wide', axis=0, tiled=True)  27.5 us
    all_gather x1, waiting for transfers between devices, per_device(): lax.all_gather(prod_primal, 'wide', axis=0, tiled=True)  26.7 us
  transfers between devices with their start and end apart: 10, of which 9 were waited for; matrix products, arithmetic and copies ran while one was open for 40% of the time, Pallas kernels for 0%

profile of v1, /device:TPU:0, one launch (start us, length us, event | category | flops | bytes accessed | tf_op | source)
XLA Modules:
  0.0 444.3 jit_solution(17135048042065690808)
XLA Ops:
  7.3 32.8 %all-gather.14.cloned.1.call-done = bf16[512,2048]{1,0:T(8,128)(2,1)} async-done(((bf16[512,256]{1,0:T(8,128)(2,1)}), bf16[512,2048]{1,0:T(8,128)(2,1)}) %all-gather.14.cloned.1.call-update) | async-done | bytes 2097168 | tf_op jit(solution)/shard_map/all_gather | solution.py:20
  40.1 3.3 broadcast_select_fusion.1
  43.4 2.8 broadcast_select_fusion
  47.1 24.4 %all-gather.30.cloned.1.call-done = bf16[1024,512]{1,0:T(8,128)(2,1)} async-done(((bf16[256,512]{1,0:T(8,128)(2,1)}), bf16[1024,512]{1,0:T(8,128)(2,1)}) %all-gather.30.cloned.1.call-update) | async-done | bytes 1048592 | tf_op jit(solution)/shard_map/all_gather | solution.py:9
  71.5 2.2 reduce_sum.37
  73.7 26.7 %all-gather.32.cloned.1.call-done = bf16[1024,512]{1,0:T(8,128)(2,1)} async-done(((bf16[256,512]{1,0:T(8,128)(2,1)}), bf16[1024,512]{1,0:T(8,128)(2,1)}) %all-gather.32.cloned.1.call-update) | async-done | bytes 1048592 | tf_op jit(solution)/shard_map/all_gather | solution.py:9
  100.5 2.1 reduce_sum.38
  104.2 25.1 %all-gather.28.cloned.1.call-done = bf16[256,2048]{1,0:T(8,128)(2,1)} async-done(((bf16[64,2048]{1,0:T(8,128)(2,1)}), bf16[256,2048]{1,0:T(8,128)(2,1)}) %all-gather.28.cloned.1.call-update) | async-done | bytes 1048592 | tf_op jit(solution)/shard_map/all_gather | solution.py:9
  130.7 27.5 %all-gather.16.cloned.1.call-done = bf16[2048,512]{1,0:T(8,128)(2,1)} async-done(((bf16[256,512]{1,0:T(8,128)(2,1)}), bf16[2048,512]{1,0:T(8,128)(2,1)}) %all-gather.16.cloned.1.call-update) | async-done | bytes 2097168 | tf_op jit(solution)/shard_map/all_gather | solution.py:44
  158.2 2.1 fusion.65
  160.3 27.5 %all-gather.18.cloned.1.call-done = bf16[2048,512]{1,0:T(8,128)(2,1)} async-done(((bf16[256,512]{1,0:T(8,128)(2,1)}), bf16[2048,512]{1,0:T(8,128)(2,1)}) %all-gather.18.cloned.1.call-update) | async-done | bytes 2097168 | tf_op jit(solution)/shard_map/all_gather | solution.py:45
  187.8 2.7 fusion.12
  190.8 26.7 %all-gather.22.cloned.1.call-done = bf16[2048,512]{1,0:T(8,128)(2,1)} async-done(((bf16[256,512]{1,0:T(8,128)(2,1)}), bf16[2048,512]{1,0:T(8,128)(2,1)}) %all-gather.22.cloned.1.call-update) | async-done | bytes 2097168 | tf_op jit(solution)/shard_map/all_gather | solution.py:30
  217.5 2.2 fusion.68
  219.7 27.5 %all-gather.24.cloned.1.call-done = bf16[2048,512]{1,0:T(8,128)(2,1)} async-done(((bf16[256,512]{1,0:T(8,128)(2,1)}), bf16[2048,512]{1,0:T(8,128)(2,1)}) %all-gather.24.cloned.1.call-update) | async-done | bytes 2097168 | tf_op jit(solution)/shard_map/all_gather | solution.py:31
  247.2 2.7 fusion.11
  249.9 6.0 %fusion.67 = f32[512,1024]{1,0:T(8,128)} fusion(bf16[2048,512]{1,0:T(8,128)(2,1)S(1)} %copy-done.7, bf16[1024,2048]{1,0:T(8,128)(2,1)} %param.4), kind=kOutput, calls=%fused_computation.112 | convolution fusion | flops 2147483648 | bytes 8388608 | tf_op jit(solution)/shard_map/dot_general | solution.py:35
  256.0 2.4 fusion.66
  258.4 3.7 multiply_multiply_fusion
  262.1 10.3 %all-gather.20.cloned.1.call-done = f32[512,512]{1,0:T(8,128)} async-done(((f32[64,512]{1,0:T(8,128)}), f32[512,512]{1,0:T(8,128)}) %all-gather.20.cloned.1.call-update) | async-done | bytes 1048592 | tf_op jit(solution)/shard_map/all_gather | solution.py:55
  275.3 11.9 %cholesky.104 = f32[128,128]{1,0:T(8,128)S(1)} custom-call(f32[128,128]{1,0:T(8,128)S(1)} %cholesky.266), custom_call_target="Cholesky" | custom-call | tf_op jit(solution)/shard_map/jit(cholesky)/cholesky | solution.py:56
  287.4 9.8 %custom-call.34 = f32[1,128,128]{1,2,0:T(8,128)S(1)} custom-call(f32[1,128,128]{2,1,0:T(8,128)S(1)} %get-tuple-element.32), custom_call_target="InvertDiagBlocksLowerTriangular" | custom-call | tf_op jit(solution)/shard_map/jit(cholesky)/cholesky | solution.py:56
  299.7 11.7 %cholesky.217 = f32[128,128]{1,0:T(8,128)S(1)} custom-call(f32[128,128]{1,0:T(8,128)S(1)} %cholesky.270), custom_call_target="Cholesky" | custom-call | tf_op jit(solution)/shard_map/jit(cholesky)/cholesky | solution.py:56
  311.5 9.8 %custom-call.35 = f32[1,128,128]{1,2,0:T(8,128)S(1)} custom-call(f32[1,128,128]{2,1,0:T(8,128)S(1)} %get-tuple-element.29), custom_call_target="InvertDiagBlocksLowerTriangular" | custom-call | tf_op jit(solution)/shard_map/jit(cholesky)/cholesky | solution.py:56
  322.9 12.1 %cholesky.238 = f32[128,128]{1,0:T(8,128)S(1)} custom-call(f32[128,128]{1,0:T(8,128)S(1)} %cholesky.275), custom_call_target="Cholesky" | custom-call | tf_op jit(solution)/shard_map/jit(cholesky)/cholesky | solution.py:56
  335.0 9.8 %custom-call.36 = f32[1,128,128]{1,2,0:T(8,128)S(1)} custom-call(f32[1,128,128]{2,1,0:T(8,128)S(1)} %get-tuple-element.26), custom_call_target="InvertDiagBlocksLowerTriangular" | custom-call | tf_op jit(solution)/shard_map/jit(cholesky)/cholesky | solution.py:56
  346.3 11.7 %cholesky.255 = f32[128,128]{1,0:T(8,128)S(1)} custom-call(f32[128,128]{1,0:T(8,128)S(1)} %convolution_subtract_fusion.7), custom_call_target="Cholesky" | custom-call | tf_op jit(solution)/shard_map/jit(cholesky)/cholesky | solution.py:56
  362.7 10.6 %while.1 = (s32[]{:T(128)}, f32[512,512]{1,0:T(8,128)S(1)}, s32[4,2]{0,1:T(2,128)S(1)}, f32[4,128,128]{2,1,0:T(8,128)}, s32[]{:T(128)}) while((s32[]{:T(128)}, f32[512,512]{1,0:T(8,128)S(1)}, s32[4,2]{0,1:T(2,128)S(1)}, f32[4,128,128]{2,1,0:T(8,128)}, s32[]{:T(128)}) %tuple.29), condition=%wide.while_cond, body=%wide.while_body.sunk | while | flops 2 | bytes 132205 | solution.py:57
  373.3 40.3 %custom-call.37 = f32[4,128,128]{1,2,0:T(8,128)S(1)} custom-call(f32[4,128,128]{2,1,0:T(8,128)} %get-tuple-element.12), custom_call_target="InvertDiagBlocksLowerTriangular" | custom-call | tf_op jit(solution)/shard_map/jit(_solve_triangular)/triangular_solve | solution.py:57
  426.9 3.6 fusion.10
  430.5 3.8 fusion
  434.3 2.9 copy.14
  (104 shorter events, 39.4 us)
Async XLA Ops:
  6.5 33.5 %copy-start = (bf16[256,2048]{1,0:T(8,128)(2,1)S(1)}, bf16[256,2048]{1,0:T(8,128)(2,1)}, u32[]{:S(2)}) copy-start(bf16[256,2048]{1,0:T(8,128)(2,1)} %param.6) | copy-start | bytes 3145732
  6.5 33.5 %all-gather.14.cloned.1.call-start = ((), (), s32[]{:S(2)}) async-start(), calls=%async_computation | async-start | bytes 2359296 | tf_op jit(solution)/shard_map/all_gather | solution.py:20
  7.3 64.3 %all-gather.30.cloned.1.call-start = ((), (), s32[]{:S(2)}) async-start(), calls=%async_computation.8 | async-start | bytes 1310720 | tf_op jit(solution)/shard_map/all_gather | solution.py:9
  40.1 3.4 copy-start.12
  43.4 57.1 %all-gather.32.cloned.1.call-start = ((), (), s32[]{:S(2)}) async-start(), calls=%async_computation.9 | async-start | bytes 1310720 | tf_op jit(solution)/shard_map/all_gather | solution.py:9
  46.2 83.1 %all-gather.28.cloned.1.call-start = ((), (), s32[]{:S(2)}) async-start(), calls=%async_computation.7 | async-start | bytes 1310720 | tf_op jit(solution)/shard_map/all_gather | solution.py:9
  47.1 111.1 %all-gather.16.cloned.1.call-start = ((), (), s32[]{:S(2)}) async-start(), calls=%async_computation.1 | async-start | bytes 2359296 | tf_op jit(solution)/shard_map/all_gather | solution.py:44
  73.7 114.1 %all-gather.18.cloned.1.call-start = ((), (), s32[]{:S(2)}) async-start(), calls=%async_computation.2 | async-start | bytes 2359296 | tf_op jit(solution)/shard_map/all_gather | solution.py:45
  102.6 114.8 %all-gather.22.cloned.1.call-start = ((), (), s32[]{:S(2)}) async-start(), calls=%async_computation.4 | async-start | bytes 2359296 | tf_op jit(solution)/shard_map/all_gather | solution.py:30
  103.4 143.8 %all-gather.24.cloned.1.call-start = ((), (), s32[]{:S(2)}) async-start(), calls=%async_computation.5 | async-start | bytes 2359296 | tf_op jit(solution)/shard_map/all_gather | solution.py:31
  104.1 168.3 %all-gather.20.cloned.1.call-start = ((), (), s32[]{:S(2)}) async-start(), calls=%async_computation.3 | async-start | bytes 1179648 | tf_op jit(solution)/shard_map/all_gather | solution.py:55
  190.5 231.1 %all-gather.26.cloned.1.call-start = ((), (), s32[]{:S(2)}) async-start(), calls=%async_computation.6 | async-start | bytes 1179648 | tf_op jit(solution)/shard_map/all_gather | solution.py:41
  217.5 32.4 %copy-start.7 = (bf16[2048,512]{1,0:T(8,128)(2,1)S(1)}, bf16[2048,512]{1,0:T(8,128)(2,1)}, u32[]{:S(2)}) copy-start(bf16[2048,512]{1,0:T(8,128)(2,1)} %all-gather.22.cloned.1.call-done) | copy-start | bytes 6291460
  249.9 6.0 %copy-start.6 = (bf16[2048,512]{1,0:T(8,128)(2,1)S(1)}, bf16[2048,512]{1,0:T(8,128)(2,1)}, u32[]{:S(2)}) copy-start(bf16[2048,512]{1,0:T(8,128)(2,1)} %all-gather.16.cloned.1.call-done) | copy-start | bytes 6291460
  249.9 6.0 %copy-start.13 = (bf16[1024,2048]{1,0:T(8,128)(2,1)S(1)}, bf16[1024,2048]{1,0:T(8,128)(2,1)}, u32[]{:S(2)}) copy-start(bf16[1024,2048]{1,0:T(8,128)(2,1)} %param.4) | copy-start | bytes 12582916
  256.0 2.4 copy-start.4
  272.4 1.7 copy-start.1
  274.3 1.0 copy-start.2
  413.6 4.1 copy-start.5
  419.1 1.1 copy-start.8
  421.7 3.2 copy-start.10
  424.4 2.4 copy-start.9
  424.5 2.4 copy-start.11
  425.8 4.7 %copy-start.15 = (f32[512,1024]{1,0:T(8,128)S(1)}, f32[512,1024]{1,0:T(8,128)}, u32[]{:S(2)}) copy-start(f32[512,1024]{1,0:T(8,128)} %fusion.67) | copy-start | bytes 6291460
  426.9 3.7 copy-start.3
  426.9 3.7 copy-start.14
Sparse Core Ops, SparseCore 0:
  9.2 30.8 all-gather.13
  43.5 27.9 all-gather.29
  73.1 27.3 all-gather.31
  101.9 27.3 all-gather.27
  131.0 27.1 all-gather.15
  160.0 27.7 all-gather.17
  189.7 27.7 all-gather.21
  219.3 27.7 all-gather.23
  249.0 23.3 all-gather.19
  274.2 23.5 all-gather.25
